TPU v7x, 32 devices: a whole 2x2x4 slice. The times are simulated.
32 devices in a mesh: inl: 4 (over x, core), xl: 8 (over z, y).
Axes of the slice: x: 2, y: 2, z: 4, core: 2. Of those that a mesh axis runs over, the one named last changes fastest.
Arguments:
- baseline: float32 [16, 128, 1024], P('inl', 'xl'), may hold values from -600 to 600
- monitor: float32 [16, 128, 1024], P('inl', 'xl'), may hold values from -900 to 900
- shift_model: float32 [4, 32, 128], P(None, None, 'xl'), may hold values from -4 to 4
- knot_start: int32 [32, 4], replicated, may hold values from -12 to 13, as said below
- half_width: int32 [8], P('xl'), may hold values from 1 to 3
Outputs:
- shift_obs: float32 [16, 128, 1024], P('inl', 'xl')
- delta: float32 [4, 32, 128], P(None, 'xl', 'inl')
Inputs may be any that keep to these rules, and one draw needn't show every extreme that they name: `knot_start`: basis function k of a window starts at sample k * 8 - 3 * 4 or one later, relative to the window's first sample.
All inputs are finite; a program needn't handle non-finite values.
Results may differ from a plain program's by a relative error of at most 0.00018.
Values sent between devices are 32-bit elements; how exact they have to be, the bound alone decides.
A program may use at most 64 MiB of HBM per device.

v0:
```python
import jax
import jax.numpy as jnp
from jax import lax
from jax.sharding import PartitionSpec as P

LAGS = 15
TWIN = 12
HMAX = 3
WINLEN = 32
KW = 4
KSTEP = 8
EPSILON = 1e-06
SHARPNESS = 6.0
DAMPING = 0.5


def extended(block, sides, width):
    for axis, dim in sides:
        count = lax.axis_size(axis)
        forward = [(i, i + 1) for i in range(count - 1)]
        backward = [(target, source) for source, target in forward]
        low = lax.ppermute(
            lax.slice_in_dim(block, block.shape[dim] - width, None, axis=dim), axis, forward
        )
        high = lax.ppermute(lax.slice_in_dim(block, 0, width, axis=dim), axis, backward)
        block = jnp.concatenate([low, block, high], axis=dim)
    return block


def spline(offset):
    square = offset * offset
    cubed = square * offset
    piece_one = cubed / 6.0
    piece_two = (-3.0 * cubed + 12.0 * square - 12.0 * offset + 4.0) / 6.0
    piece_three = (3.0 * cubed - 24.0 * square + 60.0 * offset - 44.0) / 6.0
    remain = 4.0 - offset
    piece_four = remain * remain * remain / 6.0
    result = jnp.where(offset < 4.0, piece_four, 0.0 * offset)
    result = jnp.where(offset < 3.0, piece_three, result)
    result = jnp.where(offset < 2.0, piece_two, result)
    result = jnp.where(offset < 1.0, piece_one, result)
    return jnp.where(offset < 0.0, 0.0 * offset, result)


def basis_table(knot_start):
    positions = jnp.arange(WINLEN).astype(jnp.float32)
    offset = (positions[None, None, :] - knot_start[:, :, None].astype(jnp.float32)) / KSTEP
    return spline(offset)


def solve_small(matrix, target):
    lower = [[None] * KW for _ in range(KW)]
    for column in range(KW):
        pivot = matrix[column][column]
        for inner in range(column):
            pivot = pivot - lower[column][inner] * lower[column][inner]
        lower[column][column] = jnp.sqrt(pivot)
        for target_row in range(column + 1, KW):
            entry = matrix[target_row][column]
            for inner in range(column):
                entry = entry - lower[target_row][inner] * lower[column][inner]
            lower[target_row][column] = entry / lower[column][column]
    forward = []
    for column in range(KW):
        entry = target[column]
        for inner in range(column):
            entry = entry - lower[column][inner] * forward[inner]
        forward.append(entry / lower[column][column])
    backward = [None] * KW
    for column in range(KW - 1, -1, -1):
        entry = forward[column]
        for inner in range(column + 1, KW):
            entry = entry - lower[inner][column] * backward[inner]
        backward[column] = entry / lower[column][column]
    return jnp.stack(backward)


def box_time(values):
    samples = values.shape[2]
    width = 2 * TWIN + 1
    padded = jnp.pad(values, ((0, 0), (0, 0), (TWIN, TWIN)))
    partial_sums = {1: padded}
    length = 1
    while 2 * length <= width:
        previous = partial_sums[length]
        partial_sums[2 * length] = previous[:, :, :-length] + previous[:, :, length:]
        length = 2 * length
    total = None
    begin = 0
    remain = width
    while remain > 0:
        if length <= remain:
            piece = partial_sums[length][:, :, begin : begin + samples]
            total = piece if total is None else total + piece
            begin = begin + length
            remain = remain - length
        length = length // 2
    return total


def normal_terms(resid_four, conf_four, table):
    row_count = resid_four.shape[0]
    windows = resid_four.shape[2]
    crossl = resid_four.shape[1]
    grad = jnp.einsum(
        "ixwu,wku->ikwx", conf_four * resid_four, table, precision=lax.Precision.HIGHEST
    )
    hess = jnp.einsum(
        "ixwu,wku,wju->ikjwx", conf_four, table, table, precision=lax.Precision.HIGHEST
    )
    return jnp.concatenate([grad, hess.reshape(row_count, KW * KW, windows, crossl)], axis=1)


def per_device(baseline, monitor, shift_model, knot_start, half_width):
    inline_rows = baseline.shape[0]
    slab_width = baseline.shape[1]
    samples = baseline.shape[2]
    paired = extended(jnp.stack([baseline, monitor]), (("xl", 2),), HMAX)
    base_ext = paired[0]
    moni_ext = paired[1]
    half_span = half_width[0]
    lateral = [
        (jnp.abs(offset) <= half_span).astype(jnp.float32) for offset in range(-HMAX, HMAX + 1)
    ]

    def smooth(values):
        timed = box_time(values)
        total = None
        for place, offset in enumerate(range(-HMAX, HMAX + 1)):
            term = lateral[place] * timed[:, HMAX + offset : HMAX + offset + slab_width]
            total = term if total is None else total + term
        return total

    energy_base = smooth(base_ext * base_ext)
    moni_pad = jnp.pad(moni_ext, ((0, 0), (0, 0), (LAGS, LAGS)))
    energy_mon = smooth(moni_pad * moni_pad)

    def one_lag(lag_index, running):
        total_exp, total_shift, total_corr = running
        lagged = lax.dynamic_slice_in_dim(moni_pad, lag_index, samples, 2)
        correlation = smooth(base_ext * lagged)
        energy = lax.dynamic_slice_in_dim(energy_mon, lag_index, samples, 2)
        normed = correlation / jnp.sqrt(energy_base * energy + EPSILON)
        weight_exp = jnp.exp(SHARPNESS * normed)
        lag_value = jnp.asarray(lag_index - LAGS, jnp.int32).astype(jnp.float32)
        return (
            total_exp + weight_exp,
            total_shift + lag_value * weight_exp,
            total_corr + normed * weight_exp,
        )

    first_lag = one_lag(0, (0.0 * energy_base, 0.0 * energy_base, 0.0 * energy_base))
    total_exp, total_shift, total_corr = lax.fori_loop(1, 2 * LAGS + 1, one_lag, first_lag)
    shift_obs = total_shift / total_exp
    confidence = 0.5 + 0.5 * total_corr / total_exp
    table = basis_table(knot_start)
    modelled = jnp.einsum(
        "kwx,wku->xwu", shift_model, table, precision=lax.Precision.HIGHEST
    ).reshape(slab_width, samples)
    resid = shift_obs - modelled[None]
    resid_piece = lax.all_to_all(resid, "xl", split_axis=2, concat_axis=1, tiled=True)
    conf_piece = lax.all_to_all(confidence, "xl", split_axis=2, concat_axis=1, tiled=True)
    row_count = resid_piece.shape[0]
    crossl = resid_piece.shape[1]
    owned = resid_piece.shape[2] // WINLEN
    table_own = lax.dynamic_slice_in_dim(table, lax.axis_index("xl") * owned, owned, 0)
    resid_four = resid_piece.reshape(row_count, crossl, owned, WINLEN)
    conf_four = conf_piece.reshape(row_count, crossl, owned, WINLEN)
    per_row = normal_terms(resid_four, conf_four, table_own)
    normal = jnp.sum(per_row, axis=0)
    summed = lax.psum(normal, "inl")
    share = summed.shape[2] // lax.axis_size("inl")
    summed = lax.dynamic_slice_in_dim(summed, lax.axis_index("inl") * share, share, 2)
    damping = DAMPING * inline_rows * lax.axis_size("inl")
    matrix = [
        [
            summed[KW + KW * first_k + second_k] + (damping if first_k == second_k else 0.0)
            for second_k in range(KW)
        ]
        for first_k in range(KW)
    ]
    target = [summed[first_k] for first_k in range(KW)]
    delta = solve_small(matrix, target)
    return (shift_obs, delta)


def solution(mesh):
    in_specs = (P("inl", "xl", None), P("inl", "xl", None), P(None, None, "xl"), P(), P("xl"))
    out_specs = (P("inl", "xl", None), P(None, "xl", "inl"))
    return jax.shard_map(
        per_device, mesh=mesh, in_specs=in_specs, out_specs=out_specs, check_vma=False
    )
```

profile of v0, /device:TPU:0, one launch (start us, length us, event | category | flops | bytes accessed | tf_op | source)
XLA Modules:
  0.0 127.3 jit_solution(12901075774814896960)
XLA Ops:
  0.6 1.2 pad_maximum_fusion.2
  1.9 1.3 %collective-permute-start.1 = (f32[2,4,3,1024]{3,2,1,0:T(4,128)S(1)}, f32[2,4,3,1024]{3,2,1,0:T(4,128)S(1)}, u32[]{:S(2)}, u32[]{:S(2)}) collective-permute-start(f32[2,4,3,1024]{3,2,1,0:T(4,128)S(1)} %get-tuple-element.489), channel_id=1, source_target_pairs={{1,0},{2,1},{3,2},{4,3},{5,4},{6,5},{7,6},{9,8},{10,9},{11,10},{12... | collective-permute-start | bytes 294920 | tf_op jit(solution)/shard_map/ppermute | solution.py:25
  3.2 5.5 %collective-permute-start = (f32[2,4,3,1024]{3,2,1,0:T(4,128)S(1)}, f32[2,4,3,1024]{3,2,1,0:T(4,128)S(1)}, u32[]{:S(2)}, u32[]{:S(2)}) collective-permute-start(f32[2,4,3,1024]{3,2,1,0:T(4,128)S(1)} %get-tuple-element.488), channel_id=1, source_target_pairs={{0,1},{1,2},{2,3},{3,4},{4,5},{5,6},{6,7},{8,9},{9,10},{10,11},{11... | collective-permute-start | bytes 294920 | tf_op jit(solution)/shard_map/ppermute | solution.py:22
  8.7 0.8 copy.41
  9.5 0.7 convert_element_type.72
  10.3 0.8 convolution_bitcast_fusion
  12.0 1.2 collective-permute-done
  14.6 0.5 slice_add_fusion.14
  17.4 0.5 multiply_add_fusion.2
  18.0 56.6 %while.21 = (s32[]{:T(128)}, f32[4,16,1024]{2,1,0:T(8,128)S(1)}, f32[4,16,1024]{2,1,0:T(8,128)S(1)}, f32[4,16,1024]{2,1,0:T(8,128)S(1)}, f32[]{:T(128)}, /*index...) while((s32[]{:T(128)}, f32[4,16,1024]{2,1,0:T(8,128)S(1)}, ...), condition=%wide.region_1.2_spmd, body=%wide.region_0.1_spmd.sunk | while | flops 2143487 | bytes 11726543 | solution.py:153
  74.6 1.7 %copy.36 = f32[4,16,1024]{1,0,2:T(4,128)} copy(f32[4,16,1024]{2,1,0:T(8,128)S(1)} %get-tuple-element.429) | data formatting | bytes 524288 | tf_op jit(solution)/shard_map/while | solution.py:153
  76.3 1.7 %copy.37 = f32[4,16,1024]{1,0,2:T(4,128)} copy(f32[4,16,1024]{2,1,0:T(8,128)S(1)} %get-tuple-element.430) | data formatting | bytes 524288 | tf_op jit(solution)/shard_map/while | solution.py:153
  78.1 0.8 copy.39
  78.9 2.3 %reshape.48 = f32[8,1,8192]{2,1,0:T(1,128)} reshape(f32[1024,4,16]{2,1,0:T(4,128)S(1)} %bitcast.52) | data formatting | bytes 524288
  81.2 6.1 %all-to-all-start = ((f32[8,1,8192]{2,1,0:T(1,128)}), f32[8,1,8192]{2,1,0:T(1,128)S(1)}, u32[]{:S(2)}, u32[]{:S(2)}) async-start(f32[8,1,8192]{2,1,0:T(1,128)} %reshape.48), calls=%async_computation | async-start | bytes 524288 | tf_op jit(solution)/shard_map/all_to_all | solution.py:162
  87.3 4.4 %broadcast_subtract_fusion = (f32[4,16,1024]{1,0,2:T(4,128)}, f32[4,16,1024]{1,0,2:T(4,128)S(1)}) fusion(f32[16,1024]{0,1:T(8,128)S(1)} %bitcast.55, f32[4,16,1024]{1,0,2:T(4,128)} %copy.36, f32[4,16,1024]{1,0,2:T(4,128)} %copy.37), kind=kLoop, calls=%fused_computation.31 | loop fusion | flops 131072 | bytes 1114112 | tf_op jit(solution)/shard_map/sub | solution.py:160
  91.7 3.8 %reshape.50 = f32[8,1,8192]{2,1,0:T(1,128)} reshape(f32[1024,4,16]{2,1,0:T(4,128)} %bitcast.51) | data formatting | bytes 524288
  95.5 0.6 all-to-all-done
  96.1 5.4 %all-to-all-start.1 = ((f32[8,1,8192]{2,1,0:T(1,128)}), f32[8,1,8192]{2,1,0:T(1,128)S(1)}, u32[]{:S(2)}, u32[]{:S(2)}) async-start(f32[8,1,8192]{2,1,0:T(1,128)} %reshape.50), calls=%async_computation.1 | async-start | bytes 524288 | tf_op jit(solution)/shard_map/all_to_all | solution.py:161
  101.7 1.4 %copy.50 = f32[4,16,1024]{2,1,0:T(8,128)} copy(f32[4,16,1024]{1,0,2:T(4,128)S(1)} %get-tuple-element.474) | data formatting | bytes 524288
  103.2 0.5 broadcast.174
  103.7 1.3 reduce
  105.0 1.5 %reshape.49 = f32[1024,4,16]{2,1,0:T(4,128)S(1)} reshape(f32[8,8192]{1,0:T(8,128)S(1)} %reduce) | data formatting | bytes 524288
  106.5 0.8 copy.40
  107.7 1.0 convolution_bitcast_fusion.1
  108.7 1.1 all-to-all-done.1
  109.9 1.3 reduce.1
  111.1 1.5 %reshape.51 = f32[1024,4,16]{2,1,0:T(4,128)S(1)} reshape(f32[8,8192]{1,0:T(8,128)S(1)} %reduce.1) | data formatting | bytes 524288
  112.7 0.8 copy.44
  114.2 1.6 %convolution_bitcast_fusion.2 = f32[4,4,4,128]{3,1,0,2:T(4,128)S(1)} fusion(f32[4,128,4,32]{3,2,1,0:T(4,128)S(1)} %mul.591, f32[32,4,32]{2,1,0:T(4,128)} %copy-done.2, s32[]{:T(128)S(6)} %select_n.40), kind=kOutput, calls=%fused_computation.28 | convolution fusion | flops 3145728 | bytes 303108 | tf_op jit(solution)/shard_map/ixwu,wku->ikwx/dot_general | solution.py:105
  115.9 10.5 %psum.7 = f32[20,4,128]{2,1,0:T(4,128)S(1)} all-reduce(f32[20,4,128]{2,1,0:T(4,128)S(1)} %copy.49), channel_id=1, replica_groups=mesh['inl'=4,'xl'=8] {'inl'}, use_global_device_ids=true, to_apply=%region_3.4 | all-reduce | flops 10240 | bytes 81920 | tf_op jit(solution)/shard_map/psum | solution.py:171
  126.7 0.6 pad_maximum_fusion.3
  (281 shorter events, 60.4 us)
Async XLA Ops:
  0.6 12.6 %copy-start = (f32[4,16,1024]{2,1,0:T(8,128)S(1)}, f32[4,16,1024]{2,1,0:T(8,128)}, u32[]{:S(2)}) copy-start(f32[4,16,1024]{2,1,0:T(8,128)} %param.8) | copy-start | bytes 786436
  0.6 12.6 %copy-start.1 = (f32[4,16,1024]{2,1,0:T(8,128)S(1)}, f32[4,16,1024]{2,1,0:T(8,128)}, u32[]{:S(2)}) copy-start(f32[4,16,1024]{2,1,0:T(8,128)} %param.7) | copy-start | bytes 786436
  1.9 10.1 %collective-permute-start.1 = (f32[2,4,3,1024]{3,2,1,0:T(4,128)S(1)}, f32[2,4,3,1024]{3,2,1,0:T(4,128)S(1)}, u32[]{:S(2)}, u32[]{:S(2)}) collective-permute-start(f32[2,4,3,1024]{3,2,1,0:T(4,128)S(1)} %get-tuple-element.489), channel_id=1, source_target_pairs={{1,0},{2,1},{3,2},{4,3},{5,4},{6,5},{7,6},{9,8},{10,9},{11,10},{12... | collective-permute-start | bytes 294920 | tf_op jit(solution)/shard_map/ppermute | solution.py:25
  3.2 10.0 %collective-permute-start = (f32[2,4,3,1024]{3,2,1,0:T(4,128)S(1)}, f32[2,4,3,1024]{3,2,1,0:T(4,128)S(1)}, u32[]{:S(2)}, u32[]{:S(2)}) collective-permute-start(f32[2,4,3,1024]{3,2,1,0:T(4,128)S(1)} %get-tuple-element.488), channel_id=1, source_target_pairs={{0,1},{1,2},{2,3},{3,4},{4,5},{5,6},{6,7},{8,9},{9,10},{10,11},{11... | collective-permute-start | bytes 294920 | tf_op jit(solution)/shard_map/ppermute | solution.py:22
  81.2 14.9 %all-to-all-start = ((f32[8,1,8192]{2,1,0:T(1,128)}), f32[8,1,8192]{2,1,0:T(1,128)S(1)}, u32[]{:S(2)}, u32[]{:S(2)}) async-start(f32[8,1,8192]{2,1,0:T(1,128)} %reshape.48), calls=%async_computation | async-start | bytes 524288 | tf_op jit(solution)/shard_map/all_to_all | solution.py:162
  96.1 13.8 %all-to-all-start.1 = ((f32[8,1,8192]{2,1,0:T(1,128)}), f32[8,1,8192]{2,1,0:T(1,128)S(1)}, u32[]{:S(2)}, u32[]{:S(2)}) async-start(f32[8,1,8192]{2,1,0:T(1,128)} %reshape.50), calls=%async_computation.1 | async-start | bytes 524288 | tf_op jit(solution)/shard_map/all_to_all | solution.py:161
  101.7 1.5 %copy-start.2 = (f32[32,4,32]{2,1,0:T(4,128)}, f32[32,4,32]{2,1,0:T(4,128)S(1)}, u32[]{:S(2)}) copy-start(f32[32,4,32]{2,1,0:T(4,128)S(1)} %fusion.46) | copy-start | bytes 49156
where the time goes:
time: 128 us; the launch traced here: 127 us
  other arithmetic  63.6 us (50%)
  local copies, waits for them, and re-layouts  24.9 us (19%)
  starting transfers between devices  18.3 us (14%)
  blocking collectives  10.5 us (8%)
  matrix products  3.41 us (3%)
  waiting for transfers between devices  2.93 us (2%)
  loops' own time  2.02 us (2%)
  between operations  1.66 us (1%)
    add x98, other arithmetic, box_time(): previous[:, :, :-length] + previous[:, :, length:]  21.5 us
    add x31, other arithmetic, one_lag(): total_corr + normed * weight_exp  12 us
    unnamed x12, local copies, waits for them, and re-layouts  11.3 us
    psum x1, blocking collectives, per_device(): summed = lax.psum(normal, 'inl')  10.5 us
    add x33, other arithmetic, box_time(): total = piece if total is None else total + piece  9.07 us
    all_to_all x1, starting transfers between devices, per_device(): lax.all_to_all(confidence, 'xl', split_axis=2, concat_axis=1, tiled=True)  6.08 us
    slice x33, local copies, waits for them, and re-layouts, box_time(): previous[:, :, :-length] + previous[:, :, length:]  5.94 us
    ppermute x1, starting transfers between devices, extended(): lax.ppermute(lax.slice_in_dim(block, block.shape[dim] - width, None, axis...  5.51 us
  transfers between devices with their start and end apart: 4, of which 3 were waited for; matrix products, arithmetic and copies ran while one was open for 14% of the time, Pallas kernels for 0%

commit v1 on v0

--- a/solution.py
+++ b/solution.py
@@ -12,6 +12,28 @@
 EPSILON = 1e-06
 SHARPNESS = 6.0
 DAMPING = 0.5
+
+
+def in_blocks(x, dim, peers):
+    before, after = (x.shape[:dim], x.shape[dim + 1 :])
+    return jnp.moveaxis(x.reshape(*before, peers, -1, *after), dim, 0)
+
+
+def in_order(parts, dim):
+    dims = list(parts.shape[1:])
+    dims[dim] *= parts.shape[0]
+    return jnp.moveaxis(parts, 0, dim).reshape(dims)
+
+
+def swapped_with_each(x, axis, split_dim, concat_dim):
+    count, index = (lax.axis_size(axis), lax.axis_index(axis))
+    parts = in_blocks(x, split_dim, count)
+    done = [parts[index]]
+    for lap in range(1, count):
+        sent = parts[index ^ lap]
+        done.append(lax.ppermute(sent, axis, [(i, i ^ lap) for i in range(count)]))
+    parts = jnp.stack(done)[index ^ jnp.arange(count)]
+    return in_order(parts, concat_dim)
 
 
 def extended(block, sides, width):
@@ -158,7 +180,7 @@
         "kwx,wku->xwu", shift_model, table, precision=lax.Precision.HIGHEST
     ).reshape(slab_width, samples)
     resid = shift_obs - modelled[None]
-    resid_piece = lax.all_to_all(resid, "xl", split_axis=2, concat_axis=1, tiled=True)
+    resid_piece = swapped_with_each(resid, "xl", 2, 1)
     conf_piece = lax.all_to_all(confidence, "xl", split_axis=2, concat_axis=1, tiled=True)
     row_count = resid_piece.shape[0]
     crossl = resid_piece.shape[1]

time: 128 us -> 122 us (0.953)
  local copies, waits for them, and re-layouts: 24.9 us -> 14.9 us
  starting transfers between devices: 18.3 us -> 24.2 us
  other arithmetic: 63.6 us -> 58.7 us
  waiting for transfers between devices: 2.93 us -> 7.08 us
    ppermute x0 -> x7, starting transfers between devices: none -> 13.6 us  [swapped_with_each(): done.append(lax.ppermute(sent, axis, [(i, i ^ lap) for i in range(count)]))]
    unnamed x12 -> x15, local copies, waits for them, and re-layouts: 11.3 us -> 4.7 us
    all_to_all x1 -> x0, starting transfers between devices: 5.39 us -> none  [per_device(): lax.all_to_all(resid, 'xl', split_axis=2, concat_axis=1, tiled=True)]
    ppermute x0 -> x7, waiting for transfers between devices: none -> 5.19 us  [swapped_with_each(): done.append(lax.ppermute(sent, axis, [(i, i ^ lap) for i in range(count)]))]
    sub x1, other arithmetic: 4.44 us -> 0.81 us  [per_device(): resid = shift_obs - modelled[None]]
    while x2 -> x0, local copies, waits for them, and re-layouts: 3.44 us -> none  [per_device(): lax.fori_loop(1, 2 * LAGS + 1, one_lag, first_lag)]
    ppermute x1, waiting for transfers between devices: 0.01 us -> 1.88 us  [extended(): lax.ppermute(lax.slice_in_dim(block, 0, width, axis=dim), axis, backward)]
    all_to_all x1, starting transfers between devices: 6.08 us -> 4.46 us  [per_device(): lax.all_to_all(confidence, 'xl', split_axis=2, concat_axis=1, tiled=True)]
  transfers between devices with their start and end apart: 4 -> 10, of which waited for: 3 -> 3; matrix products, arithmetic and copies ran while one was open for 14% -> 6% of each run, Pallas kernels for 0% -> 0%
where the time goes in v1:
time: 122 us
  other arithmetic  58.7 us (48%)
  starting transfers between devices  24.2 us (20%)
  local copies, waits for them, and re-layouts  14.9 us (12%)
  blocking collectives  10.5 us (9%)
  waiting for transfers between devices  7.08 us (6%)
  matrix products  2.73 us (2%)
  loops' own time  2.02 us (2%)
  between operations  1.77 us (1%)
    add x98, other arithmetic, box_time(): previous[:, :, :-length] + previous[:, :, length:]  21.5 us
    ppermute x7, starting transfers between devices, swapped_with_each(): done.append(lax.ppermute(sent, axis, [(i, i ^ lap) for i in range(count)]))  13.6 us
    add x31, other arithmetic, one_lag(): total_corr + normed * weight_exp  12 us
    psum x1, blocking collectives, per_device(): summed = lax.psum(normal, 'inl')  10.5 us
    add x33, other arithmetic, box_time(): total = piece if total is None else total + piece  9.07 us
    slice x33, local copies, waits for them, and re-layouts, box_time(): previous[:, :, :-length] + previous[:, :, length:]  5.94 us
    mul x30, other arithmetic, one_lag(): correlation = smooth(base_ext * lagged)  5.19 us
    ppermute x7, waiting for transfers between devices, swapped_with_each(): done.append(lax.ppermute(sent, axis, [(i, i ^ lap) for i in range(count)]))  5.19 us
  transfers between devices with their start and end apart: 10, of which 3 were waited for; matrix products, arithmetic and copies ran while one was open for 6% of the time, Pallas kernels for 0%

profile of v1, /device:TPU:0, one launch (start us, length us, event | category | flops | bytes accessed | tf_op | source)
XLA Modules:
  0.0 121.9 jit_solution(16617222505488802014)
XLA Ops:
  0.6 1.2 pad_maximum_fusion.2
  1.9 4.9 %collective-permute-start = (f32[2,4,3,1024]{3,2,1,0:T(4,128)S(1)}, f32[2,4,3,1024]{3,2,1,0:T(4,128)S(1)}, u32[]{:S(2)}, u32[]{:S(2)}) collective-permute-start(f32[2,4,3,1024]{3,2,1,0:T(4,128)S(1)} %get-tuple-element.486), channel_id=1, source_target_pairs={{0,1},{1,2},{2,3},{3,4},{4,5},{5,6},{6,7},{8,9},{9,10},{10,11},{11... | collective-permute-start | bytes 294920 | tf_op jit(solution)/shard_map/ppermute | solution.py:44
  6.7 1.3 %collective-permute-start.1 = (f32[2,4,3,1024]{3,2,1,0:T(4,128)S(1)}, f32[2,4,3,1024]{3,2,1,0:T(4,128)S(1)}, u32[]{:S(2)}, u32[]{:S(2)}) collective-permute-start(f32[2,4,3,1024]{3,2,1,0:T(4,128)S(1)} %get-tuple-element.487), channel_id=1, source_target_pairs={{1,0},{2,1},{3,2},{4,3},{5,4},{6,5},{7,6},{9,8},{10,9},{11,10},{12... | collective-permute-start | bytes 294920 | tf_op jit(solution)/shard_map/ppermute | solution.py:47
  8.8 0.7 convert_element_type.72
  9.5 0.8 copy.59
  10.6 0.8 convolution_bitcast_fusion
  11.7 1.9 %collective-permute-done.1 = f32[2,4,3,1024]{3,2,1,0:T(4,128)S(1)} collective-permute-done((f32[2,4,3,1024]{3,2,1,0:T(4,128)S(1)}, f32[2,4,3,1024]{3,2,1,0:T(4,128)S(1)}, u32[]{:S(2)}, u32[]{:S(2)}) %collective-permute-start.1) | collective-permute-done | bytes 98336 | tf_op jit(solution)/shard_map/ppermute | solution.py:47
  14.2 0.5 slice_add_fusion.14
  17.8 0.5 multiply_add_fusion.2
  18.4 56.6 %while.21 = (s32[]{:T(128)}, f32[4,16,1024]{2,1,0:T(8,128)S(1)}, f32[4,16,1024]{2,1,0:T(8,128)S(1)}, f32[4,16,1024]{2,1,0:T(8,128)S(1)}, f32[]{:T(128)}, /*index...) while((s32[]{:T(128)}, f32[4,16,1024]{2,1,0:T(8,128)S(1)}, ...), condition=%wide.region_1.2_spmd, body=%wide.region_0.1_spmd.sunk | while | flops 2143487 | bytes 11726543 | solution.py:175
  75.0 0.8 broadcast_subtract_fusion
  76.1 2.5 %collective-permute-start.2 = (f32[4,16,128]{2,1,0:T(8,128)S(1)}, f32[4,16,128]{2,1,0:T(8,128)S(1)}, u32[]{:S(2)}, u32[]{:S(2)}) collective-permute-start(f32[4,16,128]{2,1,0:T(8,128)S(1)} %bitcast.109), channel_id=1, source_target_pairs={{0,1},{1,0},{2,3},{3,2},{4,5},{5,4},{6,7},{7,6},{8,9},{9,8},{10,11... | collective-permute-start | bytes 98312 | tf_op jit(solution)/shard_map/ppermute | solution.py:34
  78.6 1.6 %collective-permute-start.3 = (f32[4,16,128]{2,1,0:T(8,128)S(1)}, f32[4,16,128]{2,1,0:T(8,128)S(1)}, u32[]{:S(2)}, u32[]{:S(2)}) collective-permute-start(f32[4,16,128]{2,1,0:T(8,128)S(1)} %bitcast.108), channel_id=1, source_target_pairs={{0,2},{1,3},{2,0},{3,1},{4,6},{5,7},{6,4},{7,5},{8,10},{9,11},{10,... | collective-permute-start | bytes 98312 | tf_op jit(solution)/shard_map/ppermute | solution.py:34
  80.2 2.6 %collective-permute-start.5 = (f32[4,16,128]{2,1,0:T(8,128)S(1)}, f32[4,16,128]{2,1,0:T(8,128)S(1)}, u32[]{:S(2)}, u32[]{:S(2)}) collective-permute-start(f32[4,16,128]{2,1,0:T(8,128)S(1)} %bitcast.106), channel_id=1, source_target_pairs={{0,4},{1,5},{2,6},{3,7},{4,0},{5,1},{6,2},{7,3},{8,12},{9,13},{10,... | collective-permute-start | bytes 98312 | tf_op jit(solution)/shard_map/ppermute | solution.py:34
  82.8 1.6 %collective-permute-start.6 = (f32[4,16,128]{2,1,0:T(8,128)S(1)}, f32[4,16,128]{2,1,0:T(8,128)S(1)}, u32[]{:S(2)}, u32[]{:S(2)}) collective-permute-start(f32[4,16,128]{2,1,0:T(8,128)S(1)} %bitcast.105), channel_id=1, source_target_pairs={{0,5},{1,4},{2,7},{3,6},{4,1},{5,0},{6,3},{7,2},{8,13},{9,12},{10,... | collective-permute-start | bytes 98312 | tf_op jit(solution)/shard_map/ppermute | solution.py:34
  84.4 0.8 copy.57
  85.3 2.3 %reshape.86 = f32[8,1,8192]{2,1,0:T(1,128)} reshape(f32[1024,4,16]{2,1,0:T(4,128)S(1)} %bitcast.91) | data formatting | bytes 524288
  87.6 4.5 %all-to-all-start = ((f32[8,1,8192]{2,1,0:T(1,128)}), f32[8,1,8192]{2,1,0:T(1,128)S(1)}, u32[]{:S(2)}, u32[]{:S(2)}) async-start(f32[8,1,8192]{2,1,0:T(1,128)} %reshape.86), calls=%async_computation | async-start | bytes 524288 | tf_op jit(solution)/shard_map/all_to_all | solution.py:184
  92.0 3.8 %collective-permute-start.7 = (f32[4,16,128]{2,1,0:T(8,128)S(1)}, f32[4,16,128]{2,1,0:T(8,128)S(1)}, u32[]{:S(2)}, u32[]{:S(2)}) collective-permute-start(f32[4,16,128]{2,1,0:T(8,128)S(1)} %bitcast.104), channel_id=1, source_target_pairs={{0,6},{1,7},{2,4},{3,5},{4,2},{5,3},{6,0},{7,1},{8,14},{9,15},{10,... | collective-permute-start | bytes 98312 | tf_op jit(solution)/shard_map/ppermute | solution.py:34
  95.8 1.5 %collective-permute-start.8 = (f32[4,16,128]{2,1,0:T(8,128)S(1)}, f32[4,16,128]{2,1,0:T(8,128)S(1)}, u32[]{:S(2)}, u32[]{:S(2)}) collective-permute-start(f32[4,16,128]{2,1,0:T(8,128)S(1)} %bitcast.103), channel_id=1, source_target_pairs={{0,7},{1,6},{2,5},{3,4},{4,3},{5,2},{6,1},{7,0},{8,15},{9,14},{10,... | collective-permute-start | bytes 98312 | tf_op jit(solution)/shard_map/ppermute | solution.py:34
  97.4 3.0 %collective-permute-done.7 = f32[4,16,128]{2,1,0:T(8,128)S(1)} collective-permute-done((f32[4,16,128]{2,1,0:T(8,128)S(1)}, f32[4,16,128]{2,1,0:T(8,128)S(1)}, u32[]{:S(2)}, u32[]{:S(2)}) %collective-permute-start.7) | collective-permute-done | bytes 32800 | tf_op jit(solution)/shard_map/ppermute | solution.py:34
  100.4 2.2 %collective-permute-done.8 = f32[4,16,128]{2,1,0:T(8,128)S(1)} collective-permute-done((f32[4,16,128]{2,1,0:T(8,128)S(1)}, f32[4,16,128]{2,1,0:T(8,128)S(1)}, u32[]{:S(2)}, u32[]{:S(2)}) %collective-permute-start.8) | collective-permute-done | bytes 32800 | tf_op jit(solution)/shard_map/ppermute | solution.py:34
  102.6 0.6 gather_fusion
  103.6 0.5 broadcast.209
  104.1 1.3 %reduce = f32[8,8192]{1,0:T(8,128)S(1)} reduce(f32[8,1,8192]{2,1,0:T(1,128)S(1)} %all-to-all-done, f32[]{:T(128)} %broadcast.209), dimensions={1}, to_apply=%all_to_all.11.reduce_sub_computation | reduce | bytes 524292 | tf_op jit(solution)/shard_map/all_to_all | solution.py:184
  105.4 1.5 %reshape.87 = f32[1024,4,16]{2,1,0:T(4,128)S(1)} reshape(f32[8,8192]{1,0:T(8,128)S(1)} %reduce) | data formatting | bytes 524288
  106.9 0.8 copy.58
  107.7 0.5 reshape.68
  108.4 0.9 convolution_bitcast_fusion.2
  109.3 1.0 convolution_bitcast_fusion.1
  110.5 10.5 %psum.7 = f32[20,4,128]{2,1,0:T(4,128)S(1)} all-reduce(f32[20,4,128]{2,1,0:T(4,128)S(1)} %copy.74), channel_id=1, replica_groups=mesh['inl'=4,'xl'=8] {'inl'}, use_global_device_ids=true, to_apply=%region_3.4 | all-reduce | flops 10240 | bytes 81920 | tf_op jit(solution)/shard_map/psum | solution.py:193
  121.3 0.6 pad_maximum_fusion.3
  (298 shorter events, 60.3 us)
Async XLA Ops:
  0.6 13.0 %copy-start.1 = (f32[4,16,1024]{2,1,0:T(8,128)S(1)}, f32[4,16,1024]{2,1,0:T(8,128)}, u32[]{:S(2)}) copy-start(f32[4,16,1024]{2,1,0:T(8,128)} %param.7) | copy-start | bytes 786436
  0.6 13.0 %copy-start = (f32[4,16,1024]{2,1,0:T(8,128)S(1)}, f32[4,16,1024]{2,1,0:T(8,128)}, u32[]{:S(2)}) copy-start(f32[4,16,1024]{2,1,0:T(8,128)} %param.8) | copy-start | bytes 786436
  1.9 9.9 %collective-permute-start = (f32[2,4,3,1024]{3,2,1,0:T(4,128)S(1)}, f32[2,4,3,1024]{3,2,1,0:T(4,128)S(1)}, u32[]{:S(2)}, u32[]{:S(2)}) collective-permute-start(f32[2,4,3,1024]{3,2,1,0:T(4,128)S(1)} %get-tuple-element.486), channel_id=1, source_target_pairs={{0,1},{1,2},{2,3},{3,4},{4,5},{5,6},{6,7},{8,9},{9,10},{10,11},{11... | collective-permute-start | bytes 294920 | tf_op jit(solution)/shard_map/ppermute | solution.py:44
  6.7 6.9 %collective-permute-start.1 = (f32[2,4,3,1024]{3,2,1,0:T(4,128)S(1)}, f32[2,4,3,1024]{3,2,1,0:T(4,128)S(1)}, u32[]{:S(2)}, u32[]{:S(2)}) collective-permute-start(f32[2,4,3,1024]{3,2,1,0:T(4,128)S(1)} %get-tuple-element.487), channel_id=1, source_target_pairs={{1,0},{2,1},{3,2},{4,3},{5,4},{6,5},{7,6},{9,8},{10,9},{11,10},{12... | collective-permute-start | bytes 294920 | tf_op jit(solution)/shard_map/ppermute | solution.py:47
  76.1 15.9 %collective-permute-start.2 = (f32[4,16,128]{2,1,0:T(8,128)S(1)}, f32[4,16,128]{2,1,0:T(8,128)S(1)}, u32[]{:S(2)}, u32[]{:S(2)}) collective-permute-start(f32[4,16,128]{2,1,0:T(8,128)S(1)} %bitcast.109), channel_id=1, source_target_pairs={{0,1},{1,0},{2,3},{3,2},{4,5},{5,4},{6,7},{7,6},{8,9},{9,8},{10,11... | collective-permute-start | bytes 98312 | tf_op jit(solution)/shard_map/ppermute | solution.py:34
  78.6 17.3 %collective-permute-start.3 = (f32[4,16,128]{2,1,0:T(8,128)S(1)}, f32[4,16,128]{2,1,0:T(8,128)S(1)}, u32[]{:S(2)}, u32[]{:S(2)}) collective-permute-start(f32[4,16,128]{2,1,0:T(8,128)S(1)} %bitcast.108), channel_id=1, source_target_pairs={{0,2},{1,3},{2,0},{3,1},{4,6},{5,7},{6,4},{7,5},{8,10},{9,11},{10,... | collective-permute-start | bytes 98312 | tf_op jit(solution)/shard_map/ppermute | solution.py:34
  80.2 17.1 %collective-permute-start.4 = (f32[4,16,128]{2,1,0:T(8,128)S(1)}, f32[4,16,128]{2,1,0:T(8,128)S(1)}, u32[]{:S(2)}, u32[]{:S(2)}) collective-permute-start(f32[4,16,128]{2,1,0:T(8,128)S(1)} %bitcast.107), channel_id=1, source_target_pairs={{0,3},{1,2},{2,1},{3,0},{4,7},{5,6},{6,5},{7,4},{8,11},{9,10},{10,... | collective-permute-start | bytes 98312 | tf_op jit(solution)/shard_map/ppermute | solution.py:34
  80.2 17.2 %collective-permute-start.5 = (f32[4,16,128]{2,1,0:T(8,128)S(1)}, f32[4,16,128]{2,1,0:T(8,128)S(1)}, u32[]{:S(2)}, u32[]{:S(2)}) collective-permute-start(f32[4,16,128]{2,1,0:T(8,128)S(1)} %bitcast.106), channel_id=1, source_target_pairs={{0,4},{1,5},{2,6},{3,7},{4,0},{5,1},{6,2},{7,3},{8,12},{9,13},{10,... | collective-permute-start | bytes 98312 | tf_op jit(solution)/shard_map/ppermute | solution.py:34
  82.8 14.6 %collective-permute-start.6 = (f32[4,16,128]{2,1,0:T(8,128)S(1)}, f32[4,16,128]{2,1,0:T(8,128)S(1)}, u32[]{:S(2)}, u32[]{:S(2)}) collective-permute-start(f32[4,16,128]{2,1,0:T(8,128)S(1)} %bitcast.105), channel_id=1, source_target_pairs={{0,5},{1,4},{2,7},{3,6},{4,1},{5,0},{6,3},{7,2},{8,13},{9,12},{10,... | collective-permute-start | bytes 98312 | tf_op jit(solution)/shard_map/ppermute | solution.py:34
  87.6 16.1 %all-to-all-start = ((f32[8,1,8192]{2,1,0:T(1,128)}), f32[8,1,8192]{2,1,0:T(1,128)S(1)}, u32[]{:S(2)}, u32[]{:S(2)}) async-start(f32[8,1,8192]{2,1,0:T(1,128)} %reshape.86), calls=%async_computation | async-start | bytes 524288 | tf_op jit(solution)/shard_map/all_to_all | solution.py:184
  92.0 8.4 %collective-permute-start.7 = (f32[4,16,128]{2,1,0:T(8,128)S(1)}, f32[4,16,128]{2,1,0:T(8,128)S(1)}, u32[]{:S(2)}, u32[]{:S(2)}) collective-permute-start(f32[4,16,128]{2,1,0:T(8,128)S(1)} %bitcast.104), channel_id=1, source_target_pairs={{0,6},{1,7},{2,4},{3,5},{4,2},{5,3},{6,0},{7,1},{8,14},{9,15},{10,... | collective-permute-start | bytes 98312 | tf_op jit(solution)/shard_map/ppermute | solution.py:34
  95.8 6.7 %collective-permute-start.8 = (f32[4,16,128]{2,1,0:T(8,128)S(1)}, f32[4,16,128]{2,1,0:T(8,128)S(1)}, u32[]{:S(2)}, u32[]{:S(2)}) collective-permute-start(f32[4,16,128]{2,1,0:T(8,128)S(1)} %bitcast.103), channel_id=1, source_target_pairs={{0,7},{1,6},{2,5},{3,4},{4,3},{5,2},{6,1},{7,0},{8,15},{9,14},{10,... | collective-permute-start | bytes 98312 | tf_op jit(solution)/shard_map/ppermute | solution.py:34
